TPU v7x, 32 devices: a whole 2x2x4 slice. The times are simulated.
32 devices in a mesh: grp: 2 (over y), feat: 4 (over z), samp: 4 (over x, core).
Axes of the slice: x: 2, y: 2, z: 4, core: 2. Of those that a mesh axis runs over, the one named last changes fastest.
Arguments:
- embeddings: bfloat16 [8192, 1024], P(('grp', 'samp')), parts along dimension 0, may hold values from -6 to 6
- sign_bits: int32 [4096], P('feat'), may hold values 0 or 1
- perms: int32 [4, 1024], P('feat'), may hold values from 0 to 1023, each once within a row
- gauss: float32 [4096], P('feat'), may hold values from -4 to 4
- scale: float32 [4096], P('feat'), may hold values from 0.5 to 2
- phase: float32 [4096], P('feat'), may hold values from -3.140625 to 3.140625
- basis: float32 [128, 4096], P('grp', 'feat'), parts along dimension 0, may hold values from -40 to 40
Outputs:
- basis_out: float32 [128, 4096], P('grp', 'feat'), parts along dimension 0
- projections: float32 [128, 4096], P('grp', 'samp'), parts along dimension 0
There are 2 independent parts, one for each index of `grp`. A program takes and returns all parts, laid end to end along the dimension named above; an argument that names none is the same for every part. Nothing has to cross between parts.
Inputs may be any that keep to these rules, and one draw needn't show every extreme that they name: Each row of perms names every number of 0 to 1023 once.
All inputs are finite; a program needn't handle non-finite values. No bound on the sum of `sign_bits` on one device may be relied on, other than what follows from the above.
Results may differ from a plain program's by a relative error of at most 0.0057.
Values sent between devices are 32-bit elements; how exact they have to be, the bound alone decides.
A program may use at most 64 MiB of HBM per device.

v0:
```python
import math
import jax
import jax.numpy as jnp
from jax import lax
from jax.sharding import PartitionSpec as P


def sylvester(width):
    indices = lax.iota(jnp.int32, width)
    parity = jnp.zeros((width, width), jnp.int32)
    for position in range(width.bit_length() - 1):
        row_bits = jnp.right_shift(indices[:, None], position) & 1
        col_bits = jnp.right_shift(indices[None, :], position) & 1
        parity = parity + row_bits * col_bits
    return jnp.where(parity % 2 == 0, 1.0, -1.0).astype(jnp.bfloat16)


def cholesky_step(grown, total):
    local_gram = jnp.dot(grown, grown.T, precision=lax.Precision.HIGHEST)
    gram = lax.psum(local_gram, "feat")
    lower = jnp.linalg.cholesky(gram / total)
    return jax.scipy.linalg.solve_triangular(lower, grown, lower=True)


def local(embeddings, sign_bits, perms, gauss, scale, phase, basis):
    width = embeddings.shape[1]
    rows = embeddings.shape[0]
    table = sylvester(width)
    features_total = width * lax.axis_size("feat")
    span_total = rows * lax.axis_size("samp")
    signs = (2 * sign_bits - 1).astype(jnp.bfloat16)
    first = jnp.dot(embeddings * signs, table, preferred_element_type=jnp.float32).astype(
        jnp.bfloat16
    )
    reorder = (lax.iota(jnp.int32, width)[:, None] == perms[0][None, :]).astype(jnp.bfloat16)
    picked = jnp.dot(first, reorder, preferred_element_type=jnp.float32)
    mixed = (picked * gauss).astype(jnp.bfloat16)
    freq = jnp.dot(mixed, table, preferred_element_type=jnp.float32) * scale / width + phase
    features = (math.sqrt(2.0) * jnp.cos(freq)).astype(jnp.bfloat16)
    basis_low = basis.astype(jnp.bfloat16)
    partial_scores = lax.dot_general(
        basis_low, features, (((1,), (1,)), ((), ())), preferred_element_type=jnp.float32
    )
    summed = lax.psum(partial_scores, "feat")
    projections = summed / math.sqrt(features_total)
    proj_low = projections.astype(jnp.bfloat16)
    update_part = jnp.dot(proj_low, features, preferred_element_type=jnp.float32)
    update = lax.psum(update_part, "samp")
    grown = basis + update / math.sqrt(span_total)
    basis_out = cholesky_step(grown, features_total)
    return (basis_out, projections)


def solution(mesh):
    placed = (
        P(("grp", "samp"), None),
        P("feat"),
        P("feat", None),
        P("feat"),
        P("feat"),
        P("feat"),
        P("grp", "feat"),
    )
    return jax.shard_map(
        local,
        mesh=mesh,
        in_specs=placed,
        out_specs=(P("grp", "feat"), P("grp", "samp")),
        check_vma=False,
    )
```

profile of v0, /device:TPU:0, one launch (start us, length us, event | category | flops | bytes accessed | tf_op | source)
XLA Modules:
  0.0 159.9 jit_solution(12361996061334306493)
XLA Ops:
  7.2 0.0 all-reduce.3.cloned.1.call-start
  7.3 0.7 add_convert_fusion
  8.0 1.5 iota_compare_fusion.7
  9.5 0.0 copy-start.2
  9.5 0.0 copy-start.3
  9.5 0.0 copy-start.4
  9.5 12.2 %fusion.2 = f32[1024,1024]{1,0:T(8,128)} fusion(bf16[1024,1024]{1,0:T(8,128)(2,1)} %param.7, bf16[1024]{0:T(1024)(128)(2,1)S(1)} %add_convert_fusion, s32[1024]{0:T(1024)S(1)} %get-tuple-element.2, s32[1024]{0:T(1024)S(1)} %get-tuple-element.3, s32[1024]{0:T(1024)S(1)} %get-tuple-element.4, s32[1024]{0:T(1024)S(1)} %get-tuple-element.5, ...), kind=kOutput, calls=%fused_computation.9 | convolution fusion | flops 4331667456 | bytes 7383040 | tf_op jit(solution)/shard_map/dot_general | solution.py:36
  21.7 0.0 copy-done.2
  21.7 0.0 copy-done.3
  21.7 0.0 copy-done.4
  21.7 0.0 copy-start
  21.7 22.2 %multiply_convert_fusion = bf16[1024,1024]{1,0:T(8,128)(2,1)S(1)} fusion(f32[1024,1024]{1,0:T(8,128)} %fusion.2, f32[1024]{0:T(1024)S(1)} %copy-done.2, f32[1024]{0:T(1024)S(1)} %copy-done.3, f32[1024]{0:T(1024)S(1)} %copy-done.4, s32[1024]{0:T(1024)S(1)} %get-tuple-element.2, s32[1024]{0:T(1024)S(1)} %get-tuple-element.3, s32[1024]{0:T(1024)S(1)} %get-tuple-element.4, ...), kind=kOutput, calls=%fused_computation.5 | convolution fusion | flops 2189426688 | bytes 6344704 | tf_op jit(solution)/shard_map/dot_general | solution.py:38
  44.0 0.0 copy-done
  44.0 1.5 convolution_bitcast_fusion
  45.4 0.0 all-reduce.3.cloned.1.call-update
  45.5 0.0 all-reduce.5.cloned.1.call-start
  45.5 38.1 %all-reduce.3.cloned.1.call-done = f32[64,1024]{1,0:T(8,128)} async-done(((f32[64,1024]{1,0:T(8,128)}), f32[64,1024]{1,0:T(8,128)}) %all-reduce.3.cloned.1.call-update) | async-done | bytes 262160 | tf_op jit(solution)/shard_map/psum | solution.py:44
  83.6 1.0 broadcast_multiply_fusion
  84.6 0.0 copy-start.1
  84.6 1.2 fusion.14
  85.8 0.0 all-reduce.5.cloned.1.call-update
  85.8 32.5 %all-reduce.5.cloned.1.call-done = f32[64,1024]{1,0:T(8,128)} async-done(((f32[64,1024]{1,0:T(8,128)}), f32[64,1024]{1,0:T(8,128)}) %all-reduce.5.cloned.1.call-update) | async-done | bytes 262160 | tf_op jit(solution)/shard_map/psum | solution.py:48
  118.4 1.4 fusion.18
  119.8 19.0 %psum.23 = f32[64,64]{0,1:T(8,128)S(1)} all-reduce(f32[64,64]{0,1:T(8,128)S(1)} %fusion.18), channel_id=1, replica_groups=mesh['grp'=2,'feat'=4,'samp'=4] {'feat'}, use_global_device_ids=true, to_apply=%region_2.3 | all-reduce | flops 4096 | bytes 32768 | tf_op jit(solution)/shard_map/psum | solution.py:20
  138.8 0.1 copy.10
  138.9 5.8 %cholesky.16 = f32[64,64]{1,0:T(8,128)S(1)} custom-call(f32[64,64]{1,0:T(8,128)S(1)} %fusion.21), custom_call_target="Cholesky" | custom-call | tf_op jit(solution)/shard_map/jit(cholesky)/cholesky | solution.py:21
  144.7 0.6 compare_reduce_fusion
  145.4 0.7 fusion.19
  146.1 4.9 %custom-call.7 = f32[1,64,64]{1,2,0:T(8,128)S(1)} custom-call(f32[1,64,64]{2,1,0:T(8,128)S(1)} %fusion.19), custom_call_target="InvertDiagBlocksLowerTriangular" | custom-call | tf_op jit(solution)/shard_map/jit(_solve_triangular)/triangular_solve | solution.py:22
  150.9 2.1 %fusion.17 = f32[64,1024]{1,0:T(8,128)} fusion(f32[64,1024]{1,0:T(8,128)S(1)} %copy-done, f32[64,1024]{1,0:T(8,128)} %all-reduce.5.cloned.1.call-done, f32[1,64,64]{1,2,0:T(8,128)S(1)} %custom-call.7), kind=kOutput, calls=%fused_computation.22 | convolution fusion | flops 50462720 | bytes 802816 | tf_op jit(solution)/shard_map/jit(_solve_triangular)/triangular_solve | solution.py:22
  153.0 0.0 copy-done.1
  (8 shorter events, 0.1 us)
Async XLA Ops:
  7.2 76.5 %all-reduce.3.cloned.1.call-start = ((), (), s32[]{:S(2)}) async-start(), calls=%async_computation | async-start | bytes 524288 | tf_op jit(solution)/shard_map/psum | solution.py:44
  9.5 12.3 %copy-start.2 = (f32[1024]{0:T(1024)S(1)}, f32[1024]{0:T(1024)}, u32[]{:S(2)}) copy-start(f32[1024]{0:T(1024)} %param.12) | copy-start | bytes 12292
  9.5 12.3 %copy-start.3 = (f32[1024]{0:T(1024)S(1)}, f32[1024]{0:T(1024)}, u32[]{:S(2)}) copy-start(f32[1024]{0:T(1024)} %param.11) | copy-start | bytes 12292
  9.5 12.3 %copy-start.4 = (f32[1024]{0:T(1024)S(1)}, f32[1024]{0:T(1024)}, u32[]{:S(2)}) copy-start(f32[1024]{0:T(1024)} %param.10) | copy-start | bytes 12292
  21.7 22.2 %copy-start = (f32[64,1024]{1,0:T(8,128)S(1)}, f32[64,1024]{1,0:T(8,128)}, u32[]{:S(2)}) copy-start(f32[64,1024]{1,0:T(8,128)} %param.13) | copy-start | bytes 786436
  45.5 72.9 %all-reduce.5.cloned.1.call-start = ((), (), s32[]{:S(2)}) async-start(), calls=%async_computation.1 | async-start | bytes 524288 | tf_op jit(solution)/shard_map/psum | solution.py:48
  84.6 68.4 %copy-start.1 = (f32[64,1024]{1,0:T(8,128)}, f32[64,1024]{1,0:T(8,128)S(1)}, u32[]{:S(2)}) copy-start(f32[64,1024]{1,0:T(8,128)S(1)} %broadcast_multiply_fusion) | copy-start | bytes 786436
Sparse Core Ops, SparseCore 0:
  45.6 37.9 all-reduce.2
  86.6 31.6 all-reduce.4
where the time goes:
time: 160 us
  waiting for transfers between devices  70.7 us (44%)
  matrix products  40.6 us (25%)
  blocking collectives  19 us (12%)
  other arithmetic  15.3 us (10%)
  between operations  14.2 us (9%)
    psum x1, waiting for transfers between devices, local(): summed = lax.psum(partial_scores, 'feat')  38.1 us
    psum x1, waiting for transfers between devices, local(): update = lax.psum(update_part, 'samp')  32.5 us
    dot_general x1, matrix products, local(): jnp.dot(mixed, table, preferred_element_type=jnp.float32) * scale / width  22.2 us
    psum x1, blocking collectives, cholesky_step(): gram = lax.psum(local_gram, 'feat')  19 us
    dot_general x1, matrix products, local(): picked = jnp.dot(first, reorder, preferred_element_type=jnp.float32)  12.2 us
    another operation x3, other arithmetic, cholesky_step(): lower = jnp.linalg.cholesky(gram / total)  6.52 us
    another operation x2, other arithmetic, cholesky_step(): return jax.scipy.linalg.solve_triangular(lower, grown, lower=True)  5.55 us
  transfers between devices with their start and end apart: 2, of which 2 were waited for; matrix products, arithmetic and copies ran while one was open for 0% of the time, Pallas kernels for 0%

commit v1 on v0

--- a/solution.py
+++ b/solution.py
@@ -41,7 +41,9 @@
     partial_scores = lax.dot_general(
         basis_low, features, (((1,), (1,)), ((), ())), preferred_element_type=jnp.float32
     )
-    summed = lax.psum(partial_scores, "feat")
+    summed = partial_scores
+    for hop in (1, 2):
+        summed = summed + lax.ppermute(summed, "feat", [(dev, dev ^ hop) for dev in range(4)])
     projections = summed / math.sqrt(features_total)
     proj_low = projections.astype(jnp.bfloat16)
     update_part = jnp.dot(proj_low, features, preferred_element_type=jnp.float32)

time: 160 us -> 144 us (0.900)
  waiting for transfers between devices: 70.7 us -> 50.7 us
  starting transfers between devices: 0.08 us -> 5.94 us
    psum x1 -> x0, waiting for transfers between devices: 38.1 us -> none  [local(): summed = lax.psum(partial_scores, 'feat')]
    ppermute x0 -> x2, waiting for transfers between devices: none -> 17.6 us  [local(): lax.ppermute(summed, 'feat', [(dev, dev ^ hop) for dev in range(4)])]
    ppermute x0 -> x2, starting transfers between devices: none -> 5.9 us  [local(): lax.ppermute(summed, 'feat', [(dev, dev ^ hop) for dev in range(4)])]
  transfers between devices with their start and end apart: 2 -> 3, of which waited for: 2 -> 3; matrix products, arithmetic and copies ran while one was open for 0% -> 0% of each run, Pallas kernels for 0% -> 0%
where the time goes in v1:
time: 144 us
  waiting for transfers between devices  50.7 us (35%)
  matrix products  39.9 us (28%)
  blocking collectives  19 us (13%)
  other arithmetic  14.4 us (10%)
  between operations  14.2 us (10%)
  starting transfers between devices  5.94 us (4%)
    psum x1, waiting for transfers between devices, local(): update = lax.psum(update_part, 'samp')  33.1 us
    dot_general x1, matrix products, local(): jnp.dot(mixed, table, preferred_element_type=jnp.float32) * scale / width  22.2 us
    psum x1, blocking collectives, cholesky_step(): gram = lax.psum(local_gram, 'feat')  19 us
    ppermute x2, waiting for transfers between devices, local(): lax.ppermute(summed, 'feat', [(dev, dev ^ hop) for dev in range(4)])  17.6 us
    dot_general x1, matrix products, local(): picked = jnp.dot(first, reorder, preferred_element_type=jnp.float32)  12.2 us
    another operation x3, other arithmetic, cholesky_step(): lower = jnp.linalg.cholesky(gram / total)  6.52 us
    ppermute x2, starting transfers between devices, local(): lax.ppermute(summed, 'feat', [(dev, dev ^ hop) for dev in range(4)])  5.9 us
    another operation x2, other arithmetic, cholesky_step(): return jax.scipy.linalg.solve_triangular(lower, grown, lower=True)  5.55 us
  transfers between devices with their start and end apart: 3, of which 3 were waited for; matrix products, arithmetic and copies ran while one was open for 0% of the time, Pallas kernels for 0%

profile of v1, /device:TPU:0, one launch (start us, length us, event | category | flops | bytes accessed | tf_op | source)
XLA Modules:
  0.0 144.1 jit_solution(5246537832076050729)
XLA Ops:
  7.2 0.0 all-reduce.2.cloned.1.call-start
  7.3 0.7 add_convert_fusion
  8.0 1.5 %iota_compare_fusion.7 = pred[1024,1024]{1,0:T(32,128)(4,1)S(1)} fusion(s32[1024]{0:T(1024)} %bitcast.15), kind=kLoop, calls=%fused_computation.7.clone.clone.2 | loop fusion | flops 1048576 | bytes 1052672 | tf_op jit(solution)/shard_map/dot_general | solution.py:36
  9.5 0.0 copy-start.2
  9.5 0.0 copy-start.3
  9.5 0.0 copy-start.4
  9.5 12.2 %fusion.2 = f32[1024,1024]{1,0:T(8,128)} fusion(bf16[1024,1024]{1,0:T(8,128)(2,1)} %param.7, bf16[1024]{0:T(1024)(128)(2,1)S(1)} %add_convert_fusion, s32[1024]{0:T(1024)S(1)} %get-tuple-element.2, s32[1024]{0:T(1024)S(1)} %get-tuple-element.3, s32[1024]{0:T(1024)S(1)} %get-tuple-element.4, s32[1024]{0:T(1024)S(1)} %get-tuple-element.5, ...), kind=kOutput, calls=%fused_computation.9 | convolution fusion | flops 4331667456 | bytes 7383040 | tf_op jit(solution)/shard_map/dot_general | solution.py:36
  21.7 0.0 copy-done.2
  21.7 0.0 copy-done.3
  21.7 0.0 copy-done.4
  21.7 0.0 copy-start
  21.8 22.2 %multiply_convert_fusion = bf16[1024,1024]{1,0:T(8,128)(2,1)S(1)} fusion(f32[1024,1024]{1,0:T(8,128)} %fusion.2, f32[1024]{0:T(1024)S(1)} %copy-done.2, f32[1024]{0:T(1024)S(1)} %copy-done.3, f32[1024]{0:T(1024)S(1)} %copy-done.4, s32[1024]{0:T(1024)S(1)} %get-tuple-element.2, s32[1024]{0:T(1024)S(1)} %get-tuple-element.3, s32[1024]{0:T(1024)S(1)} %get-tuple-element.4, ...), kind=kOutput, calls=%fused_computation.5 | convolution fusion | flops 2189426688 | bytes 6344704 | tf_op jit(solution)/shard_map/dot_general | solution.py:38
  44.0 0.0 copy-done
  44.0 0.8 convolution_bitcast_fusion
  44.7 3.1 %collective-permute-start = (f32[64,1024]{1,0:T(8,128)S(1)}, f32[64,1024]{1,0:T(8,128)S(1)}, u32[]{:S(2)}, u32[]{:S(2)}) collective-permute-start(f32[64,1024]{1,0:T(8,128)S(1)} %convolution_bitcast_fusion), channel_id=1, source_target_pairs={{0,4},{4,0},{8,12},{12,8},{1,5},{5,1},{9,13},{13,9},{2,6},{6,2},{1... | collective-permute-start | bytes 786440 | tf_op jit(solution)/shard_map/ppermute | solution.py:46
  47.8 6.3 %collective-permute-done = f32[64,1024]{1,0:T(8,128)S(1)} collective-permute-done((f32[64,1024]{1,0:T(8,128)S(1)}, f32[64,1024]{1,0:T(8,128)S(1)}, u32[]{:S(2)}, u32[]{:S(2)}) %collective-permute-start) | collective-permute-done | bytes 262176 | tf_op jit(solution)/shard_map/ppermute | solution.py:46
  54.2 2.8 %collective-permute-start.1 = (f32[64,1024]{1,0:T(8,128)S(1)}, f32[64,1024]{1,0:T(8,128)S(1)}, u32[]{:S(2)}, u32[]{:S(2)}) collective-permute-start(f32[64,1024]{1,0:T(8,128)S(1)} %add.99), channel_id=1, source_target_pairs={{0,8},{4,12},{8,0},{12,4},{1,9},{5,13},{9,1},{13,5},{2,10},{6,14},... | collective-permute-start | bytes 786440 | tf_op jit(solution)/shard_map/ppermute | solution.py:46
  57.0 11.3 %collective-permute-done.1 = f32[64,1024]{1,0:T(8,128)S(1)} collective-permute-done((f32[64,1024]{1,0:T(8,128)S(1)}, f32[64,1024]{1,0:T(8,128)S(1)}, u32[]{:S(2)}, u32[]{:S(2)}) %collective-permute-start.1) | collective-permute-done | bytes 262176 | tf_op jit(solution)/shard_map/ppermute | solution.py:46
  68.3 0.0 copy-start.1
  68.3 1.2 fusion.14
  69.5 0.0 all-reduce.2.cloned.1.call-update
  69.5 33.1 %all-reduce.2.cloned.1.call-done = f32[64,1024]{1,0:T(8,128)} async-done(((f32[64,1024]{1,0:T(8,128)}), f32[64,1024]{1,0:T(8,128)}) %all-reduce.2.cloned.1.call-update) | async-done | bytes 262160 | tf_op jit(solution)/shard_map/psum | solution.py:50
  102.6 1.4 fusion.18
  104.0 19.0 %psum.15 = f32[64,64]{0,1:T(8,128)S(1)} all-reduce(f32[64,64]{0,1:T(8,128)S(1)} %fusion.18), channel_id=1, replica_groups=mesh['grp'=2,'feat'=4,'samp'=4] {'feat'}, use_global_device_ids=true, to_apply=%region_1.2 | all-reduce | flops 4096 | bytes 32768 | tf_op jit(solution)/shard_map/psum | solution.py:20
  123.0 0.1 copy.10
  123.1 5.8 %cholesky.16 = f32[64,64]{1,0:T(8,128)S(1)} custom-call(f32[64,64]{1,0:T(8,128)S(1)} %fusion.21), custom_call_target="Cholesky" | custom-call | tf_op jit(solution)/shard_map/jit(cholesky)/cholesky | solution.py:21
  129.0 0.6 compare_reduce_fusion
  129.6 0.7 fusion.19
  130.3 4.9 %custom-call.7 = f32[1,64,64]{1,2,0:T(8,128)S(1)} custom-call(f32[1,64,64]{2,1,0:T(8,128)S(1)} %fusion.19), custom_call_target="InvertDiagBlocksLowerTriangular" | custom-call | tf_op jit(solution)/shard_map/jit(_solve_triangular)/triangular_solve | solution.py:22
  135.2 2.1 %fusion.17 = f32[64,1024]{1,0:T(8,128)} fusion(f32[64,1024]{1,0:T(8,128)S(1)} %copy-done, f32[64,1024]{1,0:T(8,128)} %all-reduce.2.cloned.1.call-done, f32[1,64,64]{1,2,0:T(8,128)S(1)} %custom-call.7), kind=kOutput, calls=%fused_computation.22 | convolution fusion | flops 50462720 | bytes 802816 | tf_op jit(solution)/shard_map/jit(_solve_triangular)/triangular_solve | solution.py:22
  137.3 0.0 copy-done.1
  (10 shorter events, 0.1 us)
Async XLA Ops:
  7.2 95.4 %all-reduce.2.cloned.1.call-start = ((), (), s32[]{:S(2)}) async-start(), calls=%async_computation | async-start | bytes 524288 | tf_op jit(solution)/shard_map/psum | solution.py:50
  9.5 12.3 %copy-start.2 = (f32[1024]{0:T(1024)S(1)}, f32[1024]{0:T(1024)}, u32[]{:S(2)}) copy-start(f32[1024]{0:T(1024)} %param.12) | copy-start | bytes 12292
  9.5 12.3 %copy-start.3 = (f32[1024]{0:T(1024)S(1)}, f32[1024]{0:T(1024)}, u32[]{:S(2)}) copy-start(f32[1024]{0:T(1024)} %param.11) | copy-start | bytes 12292
  9.5 12.3 %copy-start.4 = (f32[1024]{0:T(1024)S(1)}, f32[1024]{0:T(1024)}, u32[]{:S(2)}) copy-start(f32[1024]{0:T(1024)} %param.10) | copy-start | bytes 12292
  21.7 22.2 %copy-start = (f32[64,1024]{1,0:T(8,128)S(1)}, f32[64,1024]{1,0:T(8,128)}, u32[]{:S(2)}) copy-start(f32[64,1024]{1,0:T(8,128)} %param.13) | copy-start | bytes 786436
  44.7 9.4 %collective-permute-start = (f32[64,1024]{1,0:T(8,128)S(1)}, f32[64,1024]{1,0:T(8,128)S(1)}, u32[]{:S(2)}, u32[]{:S(2)}) collective-permute-start(f32[64,1024]{1,0:T(8,128)S(1)} %convolution_bitcast_fusion), channel_id=1, source_target_pairs={{0,4},{4,0},{8,12},{12,8},{1,5},{5,1},{9,13},{13,9},{2,6},{6,2},{1... | collective-permute-start | bytes 786440 | tf_op jit(solution)/shard_map/ppermute | solution.py:46
  54.2 14.1 %collective-permute-start.1 = (f32[64,1024]{1,0:T(8,128)S(1)}, f32[64,1024]{1,0:T(8,128)S(1)}, u32[]{:S(2)}, u32[]{:S(2)}) collective-permute-start(f32[64,1024]{1,0:T(8,128)S(1)} %add.99), channel_id=1, source_target_pairs={{0,8},{4,12},{8,0},{12,4},{1,9},{5,13},{9,1},{13,5},{2,10},{6,14},... | collective-permute-start | bytes 786440 | tf_op jit(solution)/shard_map/ppermute | solution.py:46
  68.3 69.0 %copy-start.1 = (f32[64,1024]{1,0:T(8,128)}, f32[64,1024]{1,0:T(8,128)S(1)}, u32[]{:S(2)}) copy-start(f32[64,1024]{1,0:T(8,128)S(1)} %add_multiply_fusion) | copy-start | bytes 786436
Sparse Core Ops, SparseCore 0:
  69.6 32.9 all-reduce.1
